TPU v7x, 256 devices: a whole 4x4x8 slice. The times are simulated.
256 devices in a mesh: dom: 16 (over y, z_lo, core), dir: 16 (over x, z_hi).
Axes of the slice: x: 4, y: 4, z: 8 (z_hi: 4, z_lo: 2; z = z_hi * 2 + z_lo), core: 2. Of those that a mesh axis runs over, the one named last changes fastest.
Arguments:
- coefficients: bfloat16 [2, 70, 32768], P(None, None, ('dom', 'dir')), may hold values from -6 to 6
- positions: float32 [3, 32768], P(None, ('dom', 'dir')), may hold values from -50 to 50
- polar: float32 [10240], P('dir'), may hold values from 0 to 1.4
- azimuth: float32 [10240], P('dir'), may hold values from -3.140625 to 3.140625
- weights: float32 [10240], P('dir'), may hold values from -4 to 4
- farmap: float32 [2, 2, 70, 10240], P(None, None, None, 'dir'), may hold values from -0.00390625 to 0.00390625
Outputs:
- coef_grad: float32 [2, 70, 32768], P(None, None, ('dom', 'dir'))
- place_grad: float32 [3, 32768], P(None, ('dom', 'dir'))
All inputs are finite; a program needn't handle non-finite values.
Results may differ from a plain program's by a relative error of at most 0.0052.
Values may be sent and summed in bfloat16 or wider, within the bound.
A program may use at most 64 MiB of HBM per device.

v0:
```python
import jax
import jax.numpy as jnp
from jax import lax
from jax.sharding import PartitionSpec as P

C = 70


def unit_vectors(polar, azimuth):
    sine_polar = jnp.sin(polar)
    return jnp.stack([sine_polar * jnp.cos(azimuth), sine_polar * jnp.sin(azimuth), jnp.cos(polar)])


def phase_tile(places, vectors):
    angles = (
        places[0][:, None] * vectors[0][None, :]
        + places[1][:, None] * vectors[1][None, :]
        + places[2][:, None] * vectors[2][None, :]
    )
    return (jnp.cos(angles).astype(jnp.bfloat16), jnp.sin(angles).astype(jnp.bfloat16))


def field_terms(coef_block, cos_tile, sin_tile):
    order_count = coef_block.shape[0] // 2
    real_rows = coef_block[:order_count]
    imag_rows = coef_block[order_count:]
    top_rows = jnp.concatenate([real_rows, imag_rows], axis=1)
    low_rows = jnp.concatenate([imag_rows, -real_rows], axis=1)
    left_side = jnp.concatenate([top_rows, low_rows], axis=0)
    right_side = jnp.concatenate([cos_tile, sin_tile], axis=0)
    return jnp.dot(left_side, right_side, preferred_element_type=jnp.float32)


def adjoint_terms(stacked, cos_tile, sin_tile):
    order_count = stacked.shape[0] // 2
    real_rows = stacked[:order_count]
    imag_rows = stacked[order_count:]
    top_rows = jnp.concatenate([real_rows, imag_rows], axis=1)
    low_rows = jnp.concatenate([imag_rows, -real_rows], axis=1)
    left_side = jnp.concatenate([top_rows, low_rows], axis=0)
    right_side = jnp.concatenate([cos_tile, sin_tile], axis=1)
    return lax.dot_general(
        left_side, right_side, (((1,), (1,)), ((), ())), preferred_element_type=jnp.float32
    )


def amplitude_parts(fields, farmap):
    order_count = fields.shape[0] // 2
    field_real = fields[:order_count][None]
    field_imag = fields[order_count:][None]
    map_real = farmap[:, 0]
    map_imag = farmap[:, 1]
    amp_real = jnp.sum(map_real * field_real - map_imag * field_imag, axis=1)
    amp_imag = jnp.sum(map_real * field_imag + map_imag * field_real, axis=1)
    return (amp_real, amp_imag)


def cotangent_from(amp_real, amp_imag, farmap, weights):
    map_real = farmap[:, 0]
    map_imag = farmap[:, 1]
    cot_real = weights * jnp.sum(
        amp_real[:, None] * map_real + amp_imag[:, None] * map_imag, axis=0
    )
    cot_imag = weights * jnp.sum(
        amp_real[:, None] * map_imag - amp_imag[:, None] * map_real, axis=0
    )
    return jnp.concatenate([cot_real, cot_imag], axis=0).astype(jnp.bfloat16)


def cotangent_rows(fields, farmap, weights):
    amp_real, amp_imag = amplitude_parts(fields, farmap)
    return cotangent_from(amp_real, amp_imag, farmap, weights)


def stacked_rows(adjoint, vectors):
    order_count = adjoint.shape[0] // 2
    widened = adjoint.astype(jnp.float32)
    scaled = [(vectors[axis_id][None, :] * widened).astype(jnp.bfloat16) for axis_id in range(3)]
    real_parts = [adjoint[:order_count]] + [item[:order_count] for item in scaled]
    imag_parts = [adjoint[order_count:]] + [item[order_count:] for item in scaled]
    return jnp.concatenate(real_parts + imag_parts, axis=0)


def gradients(output, coef_block):
    order_count = coef_block.shape[0] // 2
    real_out = output[: 4 * order_count]
    imag_out = output[4 * order_count :]
    coef_term = jnp.concatenate(
        [2.0 * real_out[:order_count], -2.0 * imag_out[:order_count]], axis=0
    )
    coef_real = coef_block[:order_count].astype(jnp.float32)
    coef_imag = coef_block[order_count:].astype(jnp.float32)
    place_terms = []
    for axis_id in range(3):
        lower_row = (axis_id + 1) * order_count
        upper_row = (axis_id + 2) * order_count
        place_terms.append(
            2.0
            * jnp.sum(
                coef_real * imag_out[lower_row:upper_row]
                + coef_imag * real_out[lower_row:upper_row],
                axis=0,
            )
        )
    return (coef_term, jnp.stack(place_terms))


def body(coefficients, positions, polar, azimuth, weights, farmap):
    own_count = coefficients.shape[2]
    own_rows = coefficients.reshape(2 * C, own_count)
    domain_rows = lax.all_gather(own_rows, "dir", axis=1, tiled=True)
    domain_places = lax.all_gather(positions, "dir", axis=1, tiled=True)
    vectors = unit_vectors(polar, azimuth)
    width_all = domain_rows.shape[1]
    width_block = 512
    blocks = width_all // width_block

    def forward_block(block_id, totals):
        offset = block_id * width_block
        coef_block = lax.dynamic_slice_in_dim(domain_rows, offset, width_block, 1)
        place_block = lax.dynamic_slice_in_dim(domain_places, offset, width_block, 1)
        cos_tile, sin_tile = phase_tile(place_block, vectors)
        return totals + field_terms(coef_block, cos_tile, sin_tile)

    partial_fields = lax.fori_loop(
        0, blocks, forward_block, jnp.zeros((2 * C, polar.shape[0]), jnp.float32)
    )
    fields = lax.psum(partial_fields, "dom")
    adjoint = cotangent_rows(fields, farmap, weights)
    stacked = stacked_rows(adjoint, vectors)

    def backward_block(block_id):
        offset = block_id * width_block
        coef_block = lax.dynamic_slice_in_dim(domain_rows, offset, width_block, 1)
        place_block = lax.dynamic_slice_in_dim(domain_places, offset, width_block, 1)
        cos_tile, sin_tile = phase_tile(place_block, vectors)
        return gradients(adjoint_terms(stacked, cos_tile, sin_tile), coef_block)

    coef_parts, place_parts = lax.map(backward_block, jnp.arange(blocks, dtype=jnp.int32))
    coef_part = jnp.moveaxis(coef_parts, 0, 1).reshape(2 * C, width_all)
    place_part = jnp.moveaxis(place_parts, 0, 1).reshape(3, width_all)
    coef_grad, place_grad = (
        lax.psum_scatter(coef_part, "dir", scatter_dimension=1, tiled=True),
        lax.psum_scatter(place_part, "dir", scatter_dimension=1, tiled=True),
    )
    return (coef_grad.reshape(2, C, own_count), place_grad)


def solution(mesh):
    placed = (
        P(None, None, ("dom", "dir")),
        P(None, ("dom", "dir")),
        P("dir"),
        P("dir"),
        P("dir"),
        P(None, None, None, "dir"),
    )
    return jax.shard_map(
        body,
        mesh=mesh,
        in_specs=placed,
        out_specs=(P(None, None, ("dom", "dir")), P(None, ("dom", "dir"))),
        check_vma=False,
    )
```

profile of v0, /device:TPU:8, one launch (start us, length us, event | category | flops | bytes accessed | tf_op | source)
XLA Modules:
  0.0 478.9 jit_solution(2724014570653692775)
XLA Ops:
  9.5 50.1 %all_gather.7 = bf16[140,2048]{1,0:T(8,128)(2,1)S(1)} all-gather(bf16[140,128]{1,0:T(8,128)(2,1)S(1)} %reshape.65), channel_id=1, replica_groups=mesh['dom'=16,'dir'=16] {'dir'}, dimensions={1}, use_global_device_ids=true | all-gather | bytes 609280 | tf_op jit(solution)/shard_map/all_gather | solution.py:111
  59.6 38.4 %all_gather.6 = f32[3,2048]{1,0:T(4,128)S(1)} all-gather(f32[3,128]{1,0:T(4,128)} %param.11), channel_id=1, replica_groups=mesh['dom'=16,'dir'=16] {'dir'}, dimensions={1}, use_global_device_ids=true | all-gather | bytes 26112 | tf_op jit(solution)/shard_map/all_gather | solution.py:112
  98.0 24.7 %while.29 = (s32[]{:T(128)}, f32[140,640]{1,0:T(8,128)S(1)}, bf16[140,2048]{1,0:T(8,128)(2,1)S(1)}, f32[3,2048]{1,0:T(4,128)S(1)}, f32[1,640]{1,0:T(1,128)S(1)},...) while((s32[]{:T(128)}, f32[140,640]{1,0:T(8,128)S(1)}, ...), condition=%wide.region_1.0_spmd.clone, body=%wide.region_0.0_spmd.clone.sunk | while | flops 189849616 | bytes 3953417 | solution.py:125
  98.2 5.4 %cosine_convert_fusion.5 = (bf16[512,640]{1,0:T(8,128)(2,1)S(1)}, bf16[512,640]{1,0:T(8,128)(2,1)S(1)}) fusion(f32[640]{0:T(1024)S(1)} %reduce.15, f32[512]{0:T(512)S(1)} %bitcast.83, f32[640]{0:T(1024)S(1)} %reduce.16, f32[512]{0:T(512)S(1)} %bitcast.82, f32[640]{0:T(1024)S(1)} %reduce.17, f32[512]{0:T(512)S(1)} %bitcast.81), kind=kLoop, calls=%fused_computation.35.clone.1 | loop fusion | flops 2293760 | bytes 1324544 | tf_op jit(solution)/shard_map/while/body/eval_jaxpr/convert_element_type | solution.py:20
  104.3 5.4 %cosine_convert_fusion.5 = (bf16[512,640]{1,0:T(8,128)(2,1)S(1)}, bf16[512,640]{1,0:T(8,128)(2,1)S(1)}) fusion(f32[640]{0:T(1024)S(1)} %reduce.15, f32[512]{0:T(512)S(1)} %bitcast.83, f32[640]{0:T(1024)S(1)} %reduce.16, f32[512]{0:T(512)S(1)} %bitcast.82, f32[640]{0:T(1024)S(1)} %reduce.17, f32[512]{0:T(512)S(1)} %bitcast.81), kind=kLoop, calls=%fused_computation.35.clone.1 | loop fusion | flops 2293760 | bytes 1324544 | tf_op jit(solution)/shard_map/while/body/eval_jaxpr/convert_element_type | solution.py:20
  110.5 5.4 %cosine_convert_fusion.5 = (bf16[512,640]{1,0:T(8,128)(2,1)S(1)}, bf16[512,640]{1,0:T(8,128)(2,1)S(1)}) fusion(f32[640]{0:T(1024)S(1)} %reduce.15, f32[512]{0:T(512)S(1)} %bitcast.83, f32[640]{0:T(1024)S(1)} %reduce.16, f32[512]{0:T(512)S(1)} %bitcast.82, f32[640]{0:T(1024)S(1)} %reduce.17, f32[512]{0:T(512)S(1)} %bitcast.81), kind=kLoop, calls=%fused_computation.35.clone.1 | loop fusion | flops 2293760 | bytes 1324544 | tf_op jit(solution)/shard_map/while/body/eval_jaxpr/convert_element_type | solution.py:20
  116.7 5.4 %cosine_convert_fusion.5 = (bf16[512,640]{1,0:T(8,128)(2,1)S(1)}, bf16[512,640]{1,0:T(8,128)(2,1)S(1)}) fusion(f32[640]{0:T(1024)S(1)} %reduce.15, f32[512]{0:T(512)S(1)} %bitcast.83, f32[640]{0:T(1024)S(1)} %reduce.16, f32[512]{0:T(512)S(1)} %bitcast.82, f32[640]{0:T(1024)S(1)} %reduce.17, f32[512]{0:T(512)S(1)} %bitcast.81), kind=kLoop, calls=%fused_computation.35.clone.1 | loop fusion | flops 2293760 | bytes 1324544 | tf_op jit(solution)/shard_map/while/body/eval_jaxpr/convert_element_type | solution.py:20
  124.3 113.6 %all-reduce.2.cloned.1.call-done = f32[140,640]{1,0:T(8,128)} async-done(((f32[140,640]{1,0:T(8,128)}), f32[140,640]{1,0:T(8,128)}) %all-reduce.2.cloned.1.call-update) | async-done | bytes 358416 | tf_op jit(solution)/shard_map/psum | solution.py:128
  237.9 1.0 fusion.32
  239.5 14.7 %maximum_maximum_fusion = bf16[560,1280]{1,0:T(8,128)(2,1)S(1)} fusion(bf16[280,640]{1,0:T(8,128)(2,1)S(1)} %maximum_negate_fusion, bf16[70,640]{1,0:T(8,128)(2,1)S(1)} %get-tuple-element.343, bf16[70,640]{1,0:T(8,128)(2,1)S(1)} %get-tuple-element.355, bf16[70,640]{1,0:T(8,128)(2,1)S(1)} %get-tuple-element.339, bf16[70,640]{1,0:T(8,128)(2,1)S(1)} %get-tuple-element.351, ...), kind=kLoop, calls=%fused_computation.48 | loop fusion | flops 18636800 | bytes 2508800 | tf_op jit(solution)/shard_map/while/body/eval_jaxpr/concatenate | solution.py:40
  254.2 35.1 %while.28 = (s32[]{:T(128)}, f32[4,140,512]{2,1,0:T(8,128)}, f32[4,3,512]{2,1,0:T(4,128)S(1)}, s32[4]{0:T(128)S(1)}, f32[3,2048]{1,0:T(4,128)S(1)}, /*index=5*/f...) while((s32[]{:T(128)}, f32[4,140,512]{2,1,0:T(8,128)}, ...), condition=%wide.region_11.12_spmd, body=%wide.region_7.11_spmd.sunk | while | flops 739566592 | bytes 7435559 | solution.py:139
  255.6 5.4 %cosine_convert_fusion.4 = (bf16[512,640]{1,0:T(8,128)(2,1)S(1)}, bf16[512,640]{1,0:T(8,128)(2,1)S(1)}) fusion(f32[640]{0:T(1024)S(1)} %reduce.12, f32[512]{0:T(512)S(1)} %bitcast.86, f32[640]{0:T(1024)S(1)} %reduce.13, f32[512]{0:T(512)S(1)} %bitcast.85, f32[640]{0:T(1024)S(1)} %reduce.14, f32[512]{0:T(512)S(1)} %bitcast.84), kind=kLoop, calls=%fused_computation.5.clone.1 | loop fusion | flops 2293760 | bytes 1324544 | tf_op jit(solution)/shard_map/while/body/eval_jaxpr/convert_element_type | solution.py:20
  264.4 5.4 %cosine_convert_fusion.4 = (bf16[512,640]{1,0:T(8,128)(2,1)S(1)}, bf16[512,640]{1,0:T(8,128)(2,1)S(1)}) fusion(f32[640]{0:T(1024)S(1)} %reduce.12, f32[512]{0:T(512)S(1)} %bitcast.86, f32[640]{0:T(1024)S(1)} %reduce.13, f32[512]{0:T(512)S(1)} %bitcast.85, f32[640]{0:T(1024)S(1)} %reduce.14, f32[512]{0:T(512)S(1)} %bitcast.84), kind=kLoop, calls=%fused_computation.5.clone.1 | loop fusion | flops 2293760 | bytes 1324544 | tf_op jit(solution)/shard_map/while/body/eval_jaxpr/convert_element_type | solution.py:20
  269.9 0.9 convolution_bitcast_fusion.2
  273.2 5.4 %cosine_convert_fusion.4 = (bf16[512,640]{1,0:T(8,128)(2,1)S(1)}, bf16[512,640]{1,0:T(8,128)(2,1)S(1)}) fusion(f32[640]{0:T(1024)S(1)} %reduce.12, f32[512]{0:T(512)S(1)} %bitcast.86, f32[640]{0:T(1024)S(1)} %reduce.13, f32[512]{0:T(512)S(1)} %bitcast.85, f32[640]{0:T(1024)S(1)} %reduce.14, f32[512]{0:T(512)S(1)} %bitcast.84), kind=kLoop, calls=%fused_computation.5.clone.1 | loop fusion | flops 2293760 | bytes 1324544 | tf_op jit(solution)/shard_map/while/body/eval_jaxpr/convert_element_type | solution.py:20
  278.6 0.9 convolution_bitcast_fusion.2
  282.0 5.4 %cosine_convert_fusion.4 = (bf16[512,640]{1,0:T(8,128)(2,1)S(1)}, bf16[512,640]{1,0:T(8,128)(2,1)S(1)}) fusion(f32[640]{0:T(1024)S(1)} %reduce.12, f32[512]{0:T(512)S(1)} %bitcast.86, f32[640]{0:T(1024)S(1)} %reduce.13, f32[512]{0:T(512)S(1)} %bitcast.85, f32[640]{0:T(1024)S(1)} %reduce.14, f32[512]{0:T(512)S(1)} %bitcast.84), kind=kLoop, calls=%fused_computation.5.clone.1 | loop fusion | flops 2293760 | bytes 1324544 | tf_op jit(solution)/shard_map/while/body/eval_jaxpr/convert_element_type | solution.py:20
  287.4 0.9 convolution_bitcast_fusion.2
  289.4 1.4 copy.23
  290.8 2.0 copy.20
  293.1 1.4 copy.27
  294.5 87.7 %reduce-scatter.7.cloned.1.call-done = f32[128,3]{1,0:T(8,128)} async-done(((f32[2048,3]{1,0:T(8,128)}), f32[128,3]{1,0:T(8,128)}) %reduce-scatter.7.cloned.1.call-update) | async-done | bytes 1552
  382.2 1.5 copy.24
  383.7 87.1 %reduce-scatter.5.cloned.1.call-done = f32[140,128]{1,0:T(8,128)} async-done(((f32[140,2048]{1,0:T(8,128)}), f32[140,128]{1,0:T(8,128)}) %reduce-scatter.5.cloned.1.call-update) | async-done | bytes 71696 | tf_op jit(solution)/shard_map/reduce_scatter | solution.py:143
  (99 shorter events, 16.6 us)
Async XLA Ops:
  7.2 230.7 %all-reduce.2.cloned.1.call-start = ((), (), s32[]{:S(2)}) async-start(), calls=%async_computation.2 | async-start | bytes 737280 | tf_op jit(solution)/shard_map/psum | solution.py:128
  98.0 25.7 %copy-start = (f32[2,2,70,640]{3,1,2,0:T(2,128)S(1)}, f32[2,2,70,640]{3,1,2,0:T(2,128)}, u32[]{:S(2)}) copy-start(f32[2,2,70,640]{3,1,2,0:T(2,128)} %param.15) | copy-start | bytes 2150404
  122.7 0.7 copy-start.1
  123.4 258.8 %reduce-scatter.7.cloned.1.call-start = ((), (), s32[]{:S(2)}) async-start(), calls=%async_computation.4 | async-start | bytes 1114112
  124.3 114.9 %copy-start.2 = (f32[640]{0:T(1024)S(1)}, f32[640]{0:T(1024)}, u32[]{:S(2)}) copy-start(f32[640]{0:T(1024)} %param.14) | copy-start | bytes 7684
  290.8 180.0 %reduce-scatter.5.cloned.1.call-start = ((), (), s32[]{:S(2)}) async-start(), calls=%async_computation.3 | async-start | bytes 1253376 | tf_op jit(solution)/shard_map/reduce_scatter | solution.py:143
Sparse Core Ops, SparseCore 0:
  123.6 114.2 all-reduce.1
  290.9 91.2 reduce-scatter.6
  385.7 85.0 reduce-scatter.4
where the time goes:
time: 479 us
  waiting for transfers between devices  288 us (60%)
  blocking collectives  88.5 us (18%)
  other arithmetic  64.2 us (13%)
  local copies, waits for them, and re-layouts  15 us (3%)
  between operations  13.9 us (3%)
  matrix products  5.45 us (1%)
    psum x1, waiting for transfers between devices, body(): fields = lax.psum(partial_fields, 'dom')  114 us
    unnamed x4, waiting for transfers between devices  87.7 us
    reduce_scatter x1, waiting for transfers between devices, body(): lax.psum_scatter(coef_part, 'dir', scatter_dimension=1, tiled=True)  87.1 us
    all_gather x1, blocking collectives, body(): domain_rows = lax.all_gather(own_rows, 'dir', axis=1, tiled=True)  50.1 us
    convert_element_type x8, other arithmetic, phase_tile(): jnp.cos(angles).astype(jnp.bfloat16)  43.5 us
    all_gather x1, blocking collectives, body(): domain_places = lax.all_gather(positions, 'dir', axis=1, tiled=True)  38.4 us
    concatenate x1, other arithmetic, adjoint_terms(): left_side = jnp.concatenate([top_rows, low_rows], axis=0)  14.7 us
  transfers between devices with their start and end apart: 3, of which 3 were waited for; matrix products, arithmetic and copies ran while one was open for 1% of the time, Pallas kernels for 0%

commit v1 on v0

--- a/solution.py
+++ b/solution.py
@@ -125,7 +125,7 @@
     partial_fields = lax.fori_loop(
         0, blocks, forward_block, jnp.zeros((2 * C, polar.shape[0]), jnp.float32)
     )
-    fields = lax.psum(partial_fields, "dom")
+    fields = jnp.sum(lax.all_gather(partial_fields, "dom"), axis=0)
     adjoint = cotangent_rows(fields, farmap, weights)
     stacked = stacked_rows(adjoint, vectors)
 

time: 479 us -> 404 us (0.84)
  waiting for transfers between devices: 288 us -> 211 us
    psum x1 -> x0, waiting for transfers between devices: 114 us -> none  [body(): fields = lax.psum(partial_fields, 'dom')]
    all_gather x0 -> x1, waiting for transfers between devices: none -> 38.8 us  [body(): fields = jnp.sum(lax.all_gather(partial_fields, 'dom'), axis=0)]
where the time goes in v1:
time: 404 us
  waiting for transfers between devices  211 us (52%)
  blocking collectives  88.5 us (22%)
  other arithmetic  67.2 us (17%)
  local copies, waits for them, and re-layouts  14.4 us (4%)
  between operations  13.9 us (3%)
  matrix products  5.48 us (1%)
    reduce_scatter x1, waiting for transfers between devices, body(): lax.psum_scatter(coef_part, 'dir', scatter_dimension=1, tiled=True)  87.2 us
    unnamed x4, waiting for transfers between devices  84.8 us
    all_gather x1, blocking collectives, body(): domain_rows = lax.all_gather(own_rows, 'dir', axis=1, tiled=True)  50.1 us
    convert_element_type x8, other arithmetic, phase_tile(): jnp.cos(angles).astype(jnp.bfloat16)  43.5 us
    all_gather x1, waiting for transfers between devices, body(): fields = jnp.sum(lax.all_gather(partial_fields, 'dom'), axis=0)  38.8 us
    all_gather x1, blocking collectives, body(): domain_places = lax.all_gather(positions, 'dir', axis=1, tiled=True)  38.4 us
    concatenate x1, other arithmetic, adjoint_terms(): left_side = jnp.concatenate([top_rows, low_rows], axis=0)  14.7 us
  transfers between devices with their start and end apart: 3, of which 3 were waited for; matrix products, arithmetic and copies ran while one was open for 1% of the time, Pallas kernels for 0%

profile of v1, /device:TPU:8, one launch (start us, length us, event | category | flops | bytes accessed | tf_op | source)
XLA Modules:
  0.0 403.7 jit_solution(872004874940989667)
XLA Ops:
  9.5 50.1 %all_gather.13 = bf16[140,2048]{1,0:T(8,128)(2,1)S(1)} all-gather(bf16[140,128]{1,0:T(8,128)(2,1)S(1)} %reshape.65), channel_id=1, replica_groups=mesh['dom'=16,'dir'=16] {'dir'}, dimensions={1}, use_global_device_ids=true | all-gather | bytes 609280 | tf_op jit(solution)/shard_map/all_gather | solution.py:111
  59.6 38.4 %all_gather.12 = f32[3,2048]{1,0:T(4,128)S(1)} all-gather(f32[3,128]{1,0:T(4,128)} %param.11), channel_id=1, replica_groups=mesh['dom'=16,'dir'=16] {'dir'}, dimensions={1}, use_global_device_ids=true | all-gather | bytes 26112 | tf_op jit(solution)/shard_map/all_gather | solution.py:112
  98.0 24.7 %while.29 = (s32[]{:T(128)}, f32[140,640]{1,0:T(8,128)S(1)}, bf16[140,2048]{1,0:T(8,128)(2,1)S(1)}, f32[3,2048]{1,0:T(4,128)S(1)}, f32[1,640]{1,0:T(1,128)S(1)},...) while((s32[]{:T(128)}, f32[140,640]{1,0:T(8,128)S(1)}, ...), condition=%wide.region_1.0_spmd.clone, body=%wide.region_0.0_spmd.clone.sunk | while | flops 189849616 | bytes 3953417 | solution.py:125
  98.2 5.4 %cosine_convert_fusion.5 = (bf16[512,640]{1,0:T(8,128)(2,1)S(1)}, bf16[512,640]{1,0:T(8,128)(2,1)S(1)}) fusion(f32[640]{0:T(1024)S(1)} %reduce.16, f32[512]{0:T(512)S(1)} %bitcast.85, f32[640]{0:T(1024)S(1)} %reduce.17, f32[512]{0:T(512)S(1)} %bitcast.84, f32[640]{0:T(1024)S(1)} %reduce.18, f32[512]{0:T(512)S(1)} %bitcast.83), kind=kLoop, calls=%fused_computation.35.clone.1 | loop fusion | flops 2293760 | bytes 1324544 | tf_op jit(solution)/shard_map/while/body/eval_jaxpr/convert_element_type | solution.py:20
  104.3 5.4 %cosine_convert_fusion.5 = (bf16[512,640]{1,0:T(8,128)(2,1)S(1)}, bf16[512,640]{1,0:T(8,128)(2,1)S(1)}) fusion(f32[640]{0:T(1024)S(1)} %reduce.16, f32[512]{0:T(512)S(1)} %bitcast.85, f32[640]{0:T(1024)S(1)} %reduce.17, f32[512]{0:T(512)S(1)} %bitcast.84, f32[640]{0:T(1024)S(1)} %reduce.18, f32[512]{0:T(512)S(1)} %bitcast.83), kind=kLoop, calls=%fused_computation.35.clone.1 | loop fusion | flops 2293760 | bytes 1324544 | tf_op jit(solution)/shard_map/while/body/eval_jaxpr/convert_element_type | solution.py:20
  110.5 5.4 %cosine_convert_fusion.5 = (bf16[512,640]{1,0:T(8,128)(2,1)S(1)}, bf16[512,640]{1,0:T(8,128)(2,1)S(1)}) fusion(f32[640]{0:T(1024)S(1)} %reduce.16, f32[512]{0:T(512)S(1)} %bitcast.85, f32[640]{0:T(1024)S(1)} %reduce.17, f32[512]{0:T(512)S(1)} %bitcast.84, f32[640]{0:T(1024)S(1)} %reduce.18, f32[512]{0:T(512)S(1)} %bitcast.83), kind=kLoop, calls=%fused_computation.35.clone.1 | loop fusion | flops 2293760 | bytes 1324544 | tf_op jit(solution)/shard_map/while/body/eval_jaxpr/convert_element_type | solution.py:20
  116.7 5.4 %cosine_convert_fusion.5 = (bf16[512,640]{1,0:T(8,128)(2,1)S(1)}, bf16[512,640]{1,0:T(8,128)(2,1)S(1)}) fusion(f32[640]{0:T(1024)S(1)} %reduce.16, f32[512]{0:T(512)S(1)} %bitcast.85, f32[640]{0:T(1024)S(1)} %reduce.17, f32[512]{0:T(512)S(1)} %bitcast.84, f32[640]{0:T(1024)S(1)} %reduce.18, f32[512]{0:T(512)S(1)} %bitcast.83), kind=kLoop, calls=%fused_computation.35.clone.1 | loop fusion | flops 2293760 | bytes 1324544 | tf_op jit(solution)/shard_map/while/body/eval_jaxpr/convert_element_type | solution.py:20
  124.3 38.8 %all-gather.4.cloned.1.call-done = f32[16,140,640]{2,1,0:T(8,128)} async-done(((f32[1,140,640]{2,1,0:T(8,128)}), f32[16,140,640]{2,1,0:T(8,128)}) %all-gather.4.cloned.1.call-update) | async-done | bytes 5734416 | tf_op jit(solution)/shard_map/all_gather | solution.py:128
  163.1 3.0 reduce_sum.78
  167.1 14.7 %maximum_maximum_fusion = bf16[560,1280]{1,0:T(8,128)(2,1)S(1)} fusion(bf16[280,640]{1,0:T(8,128)(2,1)S(1)} %maximum_negate_fusion, bf16[70,640]{1,0:T(8,128)(2,1)S(1)} %get-tuple-element.343, bf16[70,640]{1,0:T(8,128)(2,1)S(1)} %get-tuple-element.355, bf16[70,640]{1,0:T(8,128)(2,1)S(1)} %get-tuple-element.339, bf16[70,640]{1,0:T(8,128)(2,1)S(1)} %get-tuple-element.351, ...), kind=kLoop, calls=%fused_computation.48 | loop fusion | flops 18636800 | bytes 2508800 | tf_op jit(solution)/shard_map/while/body/eval_jaxpr/concatenate | solution.py:40
  181.8 35.2 %while.28 = (s32[]{:T(128)}, f32[4,140,512]{2,1,0:T(8,128)}, f32[4,3,512]{2,1,0:T(4,128)S(1)}, s32[4]{0:T(128)S(1)}, f32[3,2048]{1,0:T(4,128)S(1)}, /*index=5*/f...) while((s32[]{:T(128)}, f32[4,140,512]{2,1,0:T(8,128)}, ...), condition=%wide.region_11.12_spmd, body=%wide.region_7.11_spmd.sunk | while | flops 739566592 | bytes 7435559 | solution.py:139
  183.2 5.4 %cosine_convert_fusion.4 = (bf16[512,640]{1,0:T(8,128)(2,1)S(1)}, bf16[512,640]{1,0:T(8,128)(2,1)S(1)}) fusion(f32[640]{0:T(1024)S(1)} %reduce.13, f32[512]{0:T(512)S(1)} %bitcast.88, f32[640]{0:T(1024)S(1)} %reduce.14, f32[512]{0:T(512)S(1)} %bitcast.87, f32[640]{0:T(1024)S(1)} %reduce.15, f32[512]{0:T(512)S(1)} %bitcast.86), kind=kLoop, calls=%fused_computation.5.clone.1 | loop fusion | flops 2293760 | bytes 1324544 | tf_op jit(solution)/shard_map/while/body/eval_jaxpr/convert_element_type | solution.py:20
  188.7 0.9 convolution_bitcast_fusion.2
  192.0 5.4 %cosine_convert_fusion.4 = (bf16[512,640]{1,0:T(8,128)(2,1)S(1)}, bf16[512,640]{1,0:T(8,128)(2,1)S(1)}) fusion(f32[640]{0:T(1024)S(1)} %reduce.13, f32[512]{0:T(512)S(1)} %bitcast.88, f32[640]{0:T(1024)S(1)} %reduce.14, f32[512]{0:T(512)S(1)} %bitcast.87, f32[640]{0:T(1024)S(1)} %reduce.15, f32[512]{0:T(512)S(1)} %bitcast.86), kind=kLoop, calls=%fused_computation.5.clone.1 | loop fusion | flops 2293760 | bytes 1324544 | tf_op jit(solution)/shard_map/while/body/eval_jaxpr/convert_element_type | solution.py:20
  197.5 0.9 convolution_bitcast_fusion.2
  200.8 5.4 %cosine_convert_fusion.4 = (bf16[512,640]{1,0:T(8,128)(2,1)S(1)}, bf16[512,640]{1,0:T(8,128)(2,1)S(1)}) fusion(f32[640]{0:T(1024)S(1)} %reduce.13, f32[512]{0:T(512)S(1)} %bitcast.88, f32[640]{0:T(1024)S(1)} %reduce.14, f32[512]{0:T(512)S(1)} %bitcast.87, f32[640]{0:T(1024)S(1)} %reduce.15, f32[512]{0:T(512)S(1)} %bitcast.86), kind=kLoop, calls=%fused_computation.5.clone.1 | loop fusion | flops 2293760 | bytes 1324544 | tf_op jit(solution)/shard_map/while/body/eval_jaxpr/convert_element_type | solution.py:20
  209.6 5.4 %cosine_convert_fusion.4 = (bf16[512,640]{1,0:T(8,128)(2,1)S(1)}, bf16[512,640]{1,0:T(8,128)(2,1)S(1)}) fusion(f32[640]{0:T(1024)S(1)} %reduce.13, f32[512]{0:T(512)S(1)} %bitcast.88, f32[640]{0:T(1024)S(1)} %reduce.14, f32[512]{0:T(512)S(1)} %bitcast.87, f32[640]{0:T(1024)S(1)} %reduce.15, f32[512]{0:T(512)S(1)} %bitcast.86), kind=kLoop, calls=%fused_computation.5.clone.1 | loop fusion | flops 2293760 | bytes 1324544 | tf_op jit(solution)/shard_map/while/body/eval_jaxpr/convert_element_type | solution.py:20
  215.0 0.9 convolution_bitcast_fusion.2
  217.0 1.4 copy.23
  218.5 2.0 copy.20
  220.7 1.4 copy.27
  222.2 84.7 %reduce-scatter.7.cloned.1.call-done = f32[128,3]{1,0:T(8,128)} async-done(((f32[2048,3]{1,0:T(8,128)}), f32[128,3]{1,0:T(8,128)}) %reduce-scatter.7.cloned.1.call-update) | async-done | bytes 1552
  306.9 1.5 copy.24
  308.4 87.2 %reduce-scatter.5.cloned.1.call-done = f32[140,128]{1,0:T(8,128)} async-done(((f32[140,2048]{1,0:T(8,128)}), f32[140,128]{1,0:T(8,128)}) %reduce-scatter.5.cloned.1.call-update) | async-done | bytes 71696 | tf_op jit(solution)/shard_map/reduce_scatter | solution.py:143
  (100 shorter events, 17.1 us)
Async XLA Ops:
  7.2 155.9 %all-gather.4.cloned.1.call-start = ((), (), s32[]{:S(2)}) async-start(), calls=%async_computation.3 | async-start | bytes 6266880 | tf_op jit(solution)/shard_map/all_gather | solution.py:128
  98.0 25.7 %copy-start = (f32[2,2,70,640]{3,1,2,0:T(2,128)S(1)}, f32[2,2,70,640]{3,1,2,0:T(2,128)}, u32[]{:S(2)}) copy-start(f32[2,2,70,640]{3,1,2,0:T(2,128)} %param.15) | copy-start | bytes 2150404
  122.7 0.8 copy-start.1
  123.5 183.4 %reduce-scatter.7.cloned.1.call-start = ((), (), s32[]{:S(2)}) async-start(), calls=%async_computation.4 | async-start | bytes 1114112
  166.1 0.7 copy-start.2
  218.4 177.1 %reduce-scatter.5.cloned.1.call-start = ((), (), s32[]{:S(2)}) async-start(), calls=%async_computation.2 | async-start | bytes 1253376 | tf_op jit(solution)/shard_map/reduce_scatter | solution.py:143
Sparse Core Ops, SparseCore 0:
  123.6 39.4 all-gather.3
  218.6 88.2 reduce-scatter.6
  310.4 85.0 reduce-scatter.4
